TPU v7x, 256 devices: a whole 4x4x8 slice. The times are simulated.
256 devices in a mesh: lat: 8 (over x_hi, y), lon: 32 (over x_lo, z, core).
Axes of the slice: x: 4 (x_hi: 2, x_lo: 2; x = x_hi * 2 + x_lo), y: 4, z: 8, core: 2. Of those that a mesh axis runs over, the one named last changes fastest.
Arguments:
- tracer: float32 [100, 64, 4096], P(None, 'lat', 'lon'), may hold values from -100 to 100
- cotangent: float32 [100, 64, 4096], P(None, 'lat', 'lon'), may hold values from -6 to 6
- land_mask: int32 [64, 4096], P('lat', 'lon'), may hold values 0 or 1
- bottom: int32 [64, 4096], P('lat', 'lon'), may hold values from 25 to 100
- kappa: float32 [100], replicated, may hold values from 0.05 to 8
- w_in: bfloat16 [100, 512], replicated, may hold values from -0.625 to 0.625
- b_in: float32 [512], replicated, may hold values from -4 to 4
- w_out: bfloat16 [512, 100], replicated, may hold values from -0.25 to 0.25
- b_out: float32 [100], replicated, may hold values from 6 to 24
Outputs:
- tracer_adjoint: float32 [100, 64, 4096], P(None, 'lat', 'lon')
- grad_w_in: float32 [100, 512], replicated
- grad_b_in: float32 [512], replicated
- grad_w_out: float32 [512, 100], replicated
- grad_b_out: float32 [100], replicated
All inputs are finite; a program needn't handle non-finite values. No bound on the sum of `land_mask` on one device may be relied on, other than what follows from the above.
Results may differ from a plain program's by a relative error of at most 0.0069.
Values sent between devices are 32-bit elements; how exact they have to be, the bound alone decides.
A program may use at most 64 MiB of HBM per device.

v0:
```python
import math
import jax
import jax.numpy as jnp
from jax import lax
from jax.sharding import PartitionSpec as P

spread_coef = 0.15
level_eps = 1e-05


def with_halo(block, sides, width):
    for axis, dim in sides:
        count = lax.axis_size(axis)
        forward = [(i, i + 1) for i in range(count - 1)]
        forward.append((count - 1, 0))
        backward = [(target, source) for source, target in forward]
        low = lax.ppermute(
            lax.slice_in_dim(block, block.shape[dim] - width, None, axis=dim), axis, forward
        )
        high = lax.ppermute(lax.slice_in_dim(block, 0, width, axis=dim), axis, backward)
        block = jnp.concatenate([low, block, high], axis=dim)
    return block


def spread_local(field_pad, wet_pad):
    center = field_pad[:, 1:-1, 1:-1]
    wet_cells = wet_pad[:, 1:-1, 1:-1]
    neighbours = (
        (field_pad[:, 2:, 1:-1], wet_pad[:, 2:, 1:-1]),
        (field_pad[:, :-2, 1:-1], wet_pad[:, :-2, 1:-1]),
        (field_pad[:, 1:-1, :-2], wet_pad[:, 1:-1, :-2]),
        (field_pad[:, 1:-1, 2:], wet_pad[:, 1:-1, 2:]),
    )
    flux_total = jnp.zeros_like(center)
    for near_field, near_wet in neighbours:
        flux_total = flux_total + wet_cells * near_wet * (near_field - center)
    return center + spread_coef * flux_total


def column_solve(below, diagonal, above, right_side):

    def sweep_down(state_pair, row_items):
        ratio_prev, value_prev = state_pair
        below_row, diag_row, above_row, right_row = row_items
        pivot = diag_row - below_row * ratio_prev
        ratio_next = above_row / pivot
        value_next = (right_row - below_row * value_prev) / pivot
        return ((ratio_next, value_next), (ratio_next, value_next))

    zeros_row = jnp.zeros_like(right_side[0])
    _, (ratios, values) = lax.scan(
        sweep_down, (zeros_row, zeros_row), (below, diagonal, above, right_side), unroll=True
    )

    def sweep_up(later, row_items):
        ratio_row, value_row = row_items
        result_row = value_row - ratio_row * later
        return (result_row, result_row)

    _, solved = lax.scan(sweep_up, zeros_row, (ratios, values), reverse=True, unroll=True)
    return solved


def network(wet_tracer, radius, w_in, b_in, w_out, b_out):
    inputs = (wet_tracer / radius[:, None]).astype(jnp.bfloat16)
    pre_act = (
        lax.dot_general(w_in, inputs, (((0,), (0,)), ((), ())), preferred_element_type=jnp.float32)
        + b_in[:, None]
    )
    hidden = jax.nn.silu(pre_act).astype(jnp.bfloat16)
    logits = (
        lax.dot_general(w_out, hidden, (((0,), (0,)), ((), ())), preferred_element_type=jnp.float32)
        + b_out[:, None]
    )
    sinking = jax.nn.softplus(logits)
    return (inputs, pre_act, hidden, logits, sinking)


def coefficients(wet_cells, kappa_col, sinking):
    open_face = wet_cells * jnp.concatenate([wet_cells[1:], jnp.zeros_like(wet_cells[:1])], 0)
    down_coef = open_face * (kappa_col + sinking)
    up_coef = open_face * kappa_col
    prev_down = jnp.concatenate([jnp.zeros_like(down_coef[:1]), down_coef[:-1]], 0)
    prev_up = jnp.concatenate([jnp.zeros_like(up_coef[:1]), up_coef[:-1]], 0)
    diagonal = 1.0 + down_coef + prev_up
    return (open_face, down_coef, up_coef, prev_down, prev_up, diagonal)


def shards(tracer, cotangent, land_mask, bottom, kappa, w_in, b_in, w_out, b_out):
    level_count, lat_rows, lon_cols = tracer.shape
    column_count = lat_rows * lax.axis_size("lat") * lon_cols * lax.axis_size("lon")
    column_depth = (land_mask * bottom).astype(jnp.float32)
    stacked = jnp.concatenate([tracer, column_depth[None]], 0)
    padded = with_halo(stacked, (("lat", 1), ("lon", 2)), 1)
    lat_place = lax.axis_index("lat")
    upper_edge = jnp.where(lat_place == 0, 0.0, 1.0).astype(jnp.float32)
    lower_edge = jnp.where(lat_place == lax.axis_size("lat") - 1, 0.0, 1.0).astype(jnp.float32)
    lat_edge = jnp.concatenate(
        [upper_edge[None], jnp.ones((lat_rows,), jnp.float32), lower_edge[None]]
    )
    depth_pad = padded[-1] * lat_edge[:, None]
    level_ids = jnp.arange(level_count, dtype=jnp.float32)[:, None, None]
    wet_pad = (level_ids < depth_pad[None]).astype(jnp.float32)
    wet_cells = wet_pad[:, 1:-1, 1:-1]
    tracer_pad = padded[:level_count]
    mixed = spread_local(tracer_pad, wet_pad)
    wet_tracer = (wet_cells * tracer).reshape(level_count, -1)
    energy = lax.psum(jnp.sum(wet_tracer * wet_tracer, axis=1), ("lat", "lon"))
    radius = jnp.sqrt(energy / column_count + level_eps)
    inputs, pre_act, hidden, logits, sinking_flat = network(
        wet_tracer, radius, w_in, b_in, w_out, b_out
    )
    sinking = sinking_flat.reshape(tracer.shape)
    kappa_col = kappa[:, None, None]
    open_face, down_coef, up_coef, prev_down, prev_up, diagonal = coefficients(
        wet_cells, kappa_col, sinking
    )
    new_tracer = column_solve(-prev_down, diagonal, -up_coef, mixed)
    adjoint = column_solve(-prev_up, diagonal, -down_coef, cotangent)
    adjoint_pad = with_halo(adjoint, (("lat", 1), ("lon", 2)), 1)
    spread_back = spread_local(adjoint_pad, wet_pad)
    adjoint_next = jnp.concatenate([adjoint[1:], jnp.zeros_like(adjoint[:1])], 0)
    d_sinking = open_face * new_tracer * (adjoint_next - adjoint)
    d_logits = (d_sinking.reshape(level_count, -1) * jax.nn.sigmoid(logits)).astype(jnp.bfloat16)
    grad_out_t = lax.dot_general(
        d_logits, hidden, (((1,), (1,)), ((), ())), preferred_element_type=jnp.float32
    )
    grad_bout = jnp.sum(d_logits.astype(jnp.float32), axis=1)
    d_hidden = jnp.dot(w_out, d_logits, preferred_element_type=jnp.float32)
    gate_sig = jax.nn.sigmoid(pre_act)
    d_pre = (d_hidden * gate_sig * (1.0 + pre_act * (1.0 - gate_sig))).astype(jnp.bfloat16)
    grad_in = lax.dot_general(
        inputs, d_pre, (((1,), (1,)), ((), ())), preferred_element_type=jnp.float32
    )
    grad_bin = jnp.sum(d_pre.astype(jnp.float32), axis=1)[None]
    d_inputs = jnp.dot(w_in, d_pre, preferred_element_type=jnp.float32)
    level_part = jnp.sum(d_inputs * wet_tracer, axis=1)
    sum_in, sum_out_t, sum_bin, sum_bout, level_sum = lax.psum(
        (grad_in, grad_out_t, grad_bin, grad_bout, level_part), ("lat", "lon")
    )
    column_scale = 1.0 / math.sqrt(column_count)
    d_wet = (
        d_inputs / radius[:, None] - wet_tracer * (level_sum / (column_count * radius**3))[:, None]
    )
    tracer_adjoint = spread_back + wet_cells * d_wet.reshape(tracer.shape)
    grad_w_in = sum_in * column_scale
    grad_b_in = sum_bin[0] * column_scale
    grad_w_out = sum_out_t.T * column_scale
    grad_b_out = sum_bout * column_scale
    return (tracer_adjoint, grad_w_in, grad_b_in, grad_w_out, grad_b_out)


def solution(mesh):
    placed = (
        P(None, "lat", "lon"),
        P(None, "lat", "lon"),
        P("lat", "lon"),
        P("lat", "lon"),
        P(),
        P(),
        P(),
        P(),
        P(),
    )
    return jax.shard_map(
        shards,
        mesh=mesh,
        in_specs=placed,
        out_specs=(P(None, "lat", "lon"), P(), P(), P(), P()),
        check_vma=False,
    )
```

profile of v0, /device:TPU:2, one launch (start us, length us, event | category | flops | bytes accessed | tf_op | source)
XLA Modules:
  0.0 479.5 jit_solution(435788746220451003)
XLA Ops:
  7.2 0.7 convert_bitcast_fusion
  7.9 1.2 pad_maximum_fusion.23
  9.1 1.7 collective-permute-start
  10.8 4.1 collective-permute-start.1
  14.9 2.1 collective-permute-done
  16.9 1.2 pad_maximum_fusion
  18.1 0.3 fusion.831
  18.4 0.4 copy.1020
  18.8 0.4 copy.1021
  19.2 4.3 collective-permute-start.3
  23.6 0.8 collective-permute-done.2
  24.4 0.5 copy.1022
  24.9 0.5 copy.1023
  25.4 0.9 copy-done.2
  26.3 0.2 fusion.7
  26.5 0.2 slice.3031
  26.7 0.7 copy-done.4
  27.5 2.3 fusion.735
  29.9 0.8 copy.1030
  30.7 81.1 %psum.42 = f32[100]{0:T(128)S(1)} all-reduce(f32[100]{0:T(128)S(1)} %get-tuple-element.618), channel_id=1, replica_groups=mesh['lat'=8,'lon'=32] {'lat','lon'}, use_global_device_ids=true, to_apply=%region_1.2 | all-reduce | flops 100 | bytes 800 | tf_op jit(solution)/shard_map/psum | solution.py:108
  111.8 1.9 fusion.5
  113.7 0.6 compare_select_fusion
  114.5 0.2 copy-done.9
  114.8 0.3 add_add_fusion
  115.2 0.3 multiply_subtract_fusion.9
  115.6 0.5 fusion.146
  116.3 1.1 fusion.15
  117.4 0.2 subtract_divide_fusion.1
  117.5 0.3 fusion.148
  117.8 0.3 fusion.49
  118.1 0.4 constant_dynamic-update-slice_fusion.199
  119.0 0.7 constant_dynamic-update-slice_fusion.162
  120.4 0.3 multiply_subtract_fusion.147
  120.8 0.5 bitcast_subtract_fusion.33
  121.4 0.2 subtract_divide_fusion.4
  121.5 0.3 fusion.411
  121.8 0.3 fusion.345
  122.1 0.4 constant_dynamic-update-slice_fusion.298
  122.9 0.7 constant_dynamic-update-slice_fusion.262
  124.4 0.2 subtract_multiply_fusion
  124.8 0.2 convert_reduce_fusion.1
  125.0 1.0 fusion.834
  126.0 1.0 convert_reduce_fusion
  127.1 1.0 copy-done.10
  128.0 1.0 fusion.543
  129.1 2.5 multiply_reduce_fusion
  131.6 1.5 collective-permute-start.4
  133.1 0.6 collective-permute-start.5
  133.7 76.5 %all-reduce.4 = (f32[100]{0:T(128)S(1)}, f32[1,512]{1,0:T(1,128)S(1)}, f32[100]{0:T(128)S(1)}) all-reduce(f32[100]{0:T(128)S(1)} %get-tuple-element.826, f32[1,512]{1,0:T(1,128)S(1)} %bitcast.5569, f32[100]{0:T(128)S(1)} %get-tuple-element.15), channel_id=1, replica_groups=mesh['lat'=8,'lon'=32] {'lat','lon'}, use_global_device_ids=true, to_apply=%region_3.4 | all-reduce | flops 712 | bytes 5696 | tf_op jit(solution)/shard_map/psum | solution.py:138
  210.3 1.1 multiply_subtract_fusion
  211.4 0.6 broadcast_multiply_fusion.2
  212.0 0.2 pad_maximum_fusion.1
  212.2 1.2 fusion.832
  213.3 1.5 copy.1024
  214.9 0.4 copy.1026
  215.3 3.9 collective-permute-start.7
  219.1 0.5 broadcast_multiply_fusion.3
  219.6 0.9 copy.1033
  220.5 0.5 copy.1025
  221.0 1.3 copy.1027
  222.3 3.0 fusion.9
  225.3 244.1 %all-reduce.8.cloned.1.call-done = (f32[100,512]{1,0:T(8,128)}, f32[100,512]{1,0:T(8,128)}) async-done(((f32[100,512]{1,0:T(8,128)}, f32[100,512]{1,0:T(8,128)}), (f32[100,512]{1,0:T(8,128)}, f32[100,512]{1,0:T(8,128)})) %all-reduce.8.cloned.1.call-update) | async-done | bytes 409616 | tf_op jit(solution)/shard_map/psum | solution.py:138
  469.3 1.6 broadcast_multiply_fusion.1
  471.0 1.6 multiply_bitcast_fusion
  (248 shorter events, 2.1 us)
Async XLA Ops:
  7.2 104.6 %copy-start = (bf16[100,512]{1,0:T(8,128)(2,1)S(1)}, bf16[100,512]{1,0:T(8,128)(2,1)}, u32[]{:S(2)}) copy-start(bf16[100,512]{1,0:T(8,128)(2,1)} %param.14) | copy-start | bytes 307204
  7.2 462.2 %all-reduce.8.cloned.1.call-start = ((), (), s32[]{:S(2)}) async-start(), calls=%async_computation | async-start | bytes 851968 | tf_op jit(solution)/shard_map/psum | solution.py:138
  9.1 7.8 %collective-permute-start = (f32[101,1,128]{2,1,0:T(1,128)S(1)}, f32[101,1,128]{2,1,0:T(1,128)S(1)}, u32[]{:S(2)}, u32[]{:S(2)}) collective-permute-start(f32[101,1,128]{2,1,0:T(1,128)S(1)} %get-tuple-element.624), channel_id=1, source_target_pairs={{0,32},{32,64},{64,96},{96,128},{128,160},{160,192},{192,224},{224... | collective-permute-start | bytes 155144 | tf_op jit(solution)/shard_map/ppermute | solution.py:17
  10.8 6.2 %collective-permute-start.1 = (f32[101,1,128]{2,1,0:T(1,128)S(1)}, f32[101,1,128]{2,1,0:T(1,128)S(1)}, u32[]{:S(2)}, u32[]{:S(2)}) collective-permute-start(f32[101,1,128]{2,1,0:T(1,128)S(1)} %get-tuple-element.625), channel_id=1, source_target_pairs={{32,0},{64,32},{96,64},{128,96},{160,128},{192,160},{224,192},{0,2... | collective-permute-start | bytes 155144 | tf_op jit(solution)/shard_map/ppermute | solution.py:20
  18.4 7.9 %copy-start.1 = (f32[100,8,128]{2,1,0:T(8,128)S(1)}, f32[100,8,128]{2,1,0:T(8,128)}, u32[]{:S(2)}) copy-start(f32[100,8,128]{2,1,0:T(8,128)} %param.9) | copy-start | bytes 1228804
  18.8 5.6 %collective-permute-start.2 = (f32[101,10,1]{0,1,2:T(8,128)S(1)}, f32[101,10,1]{0,1,2:T(8,128)S(1)}, u32[]{:S(2)}, u32[]{:S(2)}) collective-permute-start(f32[101,10,1]{0,1,2:T(8,128)S(1)} %copy.1020), channel_id=1, source_target_pairs={{0,1},{1,2},{2,3},{3,4},{4,5},{5,6},{6,7},{7,8},{8,9},{9,10},{10,1... | collective-permute-start | bytes 12128 | tf_op jit(solution)/shard_map/ppermute | solution.py:17
  19.2 5.6 %collective-permute-start.3 = (f32[101,10,1]{0,1,2:T(8,128)S(1)}, f32[101,10,1]{0,1,2:T(8,128)S(1)}, u32[]{:S(2)}, u32[]{:S(2)}) collective-permute-start(f32[101,10,1]{0,1,2:T(8,128)S(1)} %copy.1021), channel_id=1, source_target_pairs={{1,0},{2,1},{3,2},{4,3},{5,4},{6,5},{7,6},{8,7},{9,8},{10,9},{11,1... | collective-permute-start | bytes 12128 | tf_op jit(solution)/shard_map/ppermute | solution.py:20
  25.4 0.9 copy-start.2
  26.3 1.2 copy-start.11
  26.7 0.8 copy-start.4
  27.5 84.3 %copy-start.13 = (f32[512]{0:T(512)S(1)}, f32[512]{0:T(512)}, u32[]{:S(2)}) copy-start(f32[512]{0:T(512)} %param.15) | copy-start | bytes 6148
  111.8 1.9 copy-start.12
  111.8 1.9 copy-start.14
  113.7 1.0 copy-start.9
  113.7 1.1 copy-start.5
  115.2 1.1 copy-start.3
  119.0 2.4 copy-start.7
  126.0 2.0 copy-start.6
  127.0 1.0 copy-start.10
  131.6 80.4 %collective-permute-start.4 = (f32[100,1,128]{2,1,0:T(1,128)S(1)}, f32[100,1,128]{2,1,0:T(1,128)S(1)}, u32[]{:S(2)}, u32[]{:S(2)}) collective-permute-start(f32[100,1,128]{2,1,0:T(1,128)S(1)} %get-tuple-element.627), channel_id=1, source_target_pairs={{32,0},{64,32},{96,64},{128,96},{160,128},{192,160},{224,192},{0,2... | collective-permute-start | bytes 153608 | tf_op jit(solution)/shard_map/ppermute | solution.py:20
  133.1 78.9 %collective-permute-start.5 = (f32[100,1,128]{2,1,0:T(1,128)S(1)}, f32[100,1,128]{2,1,0:T(1,128)S(1)}, u32[]{:S(2)}, u32[]{:S(2)}) collective-permute-start(f32[100,1,128]{2,1,0:T(1,128)S(1)} %get-tuple-element.626), channel_id=1, source_target_pairs={{0,32},{32,64},{64,96},{96,128},{128,160},{160,192},{192,224},{224... | collective-permute-start | bytes 153608 | tf_op jit(solution)/shard_map/ppermute | solution.py:17
  214.8 5.7 %collective-permute-start.6 = (f32[100,10,1]{0,1,2:T(8,128)S(1)}, f32[100,10,1]{0,1,2:T(8,128)S(1)}, u32[]{:S(2)}, u32[]{:S(2)}) collective-permute-start(f32[100,10,1]{0,1,2:T(8,128)S(1)} %copy.1024), channel_id=1, source_target_pairs={{0,1},{1,2},{2,3},{3,4},{4,5},{5,6},{6,7},{7,8},{8,9},{9,10},{10,1... | collective-permute-start | bytes 12008 | tf_op jit(solution)/shard_map/ppermute | solution.py:17
  215.3 5.7 %collective-permute-start.7 = (f32[100,10,1]{0,1,2:T(8,128)S(1)}, f32[100,10,1]{0,1,2:T(8,128)S(1)}, u32[]{:S(2)}, u32[]{:S(2)}) collective-permute-start(f32[100,10,1]{0,1,2:T(8,128)S(1)} %copy.1026), channel_id=1, source_target_pairs={{1,0},{2,1},{3,2},{4,3},{5,4},{6,5},{7,6},{8,7},{9,8},{10,9},{11,1... | collective-permute-start | bytes 12008 | tf_op jit(solution)/shard_map/ppermute | solution.py:20
  220.5 1.8 copy-start.8
Sparse Core Ops, SparseCore 0:
  220.7 248.6 all-reduce.7
where the time goes:
time: 480 us; the launch traced here: 479 us
  waiting for transfers between devices  247 us (51%)
  blocking collectives  158 us (33%)
  other arithmetic  22.1 us (5%)
  starting transfers between devices  16.1 us (3%)
  between operations  15.9 us (3%)
  local copies, waits for them, and re-layouts  12.7 us (3%)
  matrix products  8.1 us (2%)
    psum x1, waiting for transfers between devices, shards(): lax.psum((grad_in, grad_out_t, grad_bin, grad_bout, level_part), ('lat',...  244 us
    psum x1, blocking collectives, shards(): energy = lax.psum(jnp.sum(wet_tracer * wet_tracer, axis=1), ('lat', 'lon'))  81.1 us
    psum x1, blocking collectives, shards(): lax.psum((grad_in, grad_out_t, grad_bin, grad_bout, level_part), ('lat',...  76.5 us
    ppermute x4, starting transfers between devices, with_halo(): lax.ppermute(lax.slice_in_dim(block, 0, width, axis=dim), axis, backward)  13.7 us
  transfers between devices with their start and end apart: 9, of which 3 were waited for; matrix products, arithmetic and copies ran while one was open for 2% of the time, Pallas kernels for 0%

commit v1 on v0

--- a/solution.py
+++ b/solution.py
@@ -105,7 +105,9 @@
     tracer_pad = padded[:level_count]
     mixed = spread_local(tracer_pad, wet_pad)
     wet_tracer = (wet_cells * tracer).reshape(level_count, -1)
-    energy = lax.psum(jnp.sum(wet_tracer * wet_tracer, axis=1), ("lat", "lon"))
+    energy = jnp.sum(
+        lax.all_gather(jnp.sum(wet_tracer * wet_tracer, axis=1), ("lat", "lon")), axis=0
+    )
     radius = jnp.sqrt(energy / column_count + level_eps)
     inputs, pre_act, hidden, logits, sinking_flat = network(
         wet_tracer, radius, w_in, b_in, w_out, b_out

time: 480 us -> 649 us (1.35)
  waiting for transfers between devices: 247 us -> 489 us
  blocking collectives: 158 us -> 75.9 us
    unnamed x1 -> x3, waiting for transfers between devices: 0.02 us -> 242 us
    psum x1 -> x0, blocking collectives: 81.1 us -> none  [shards(): energy = lax.psum(jnp.sum(wet_tracer * wet_tracer, axis=1), ('lat', 'lon'))]
  transfers between devices with their start and end apart: 9 -> 10, of which waited for: 3 -> 4; matrix products, arithmetic and copies ran while one was open for 2% -> 2% of each run, Pallas kernels for 0% -> 0%
where the time goes in v1:
time: 649 us
  waiting for transfers between devices  489 us (75%)
  blocking collectives  75.9 us (12%)
  other arithmetic  24.2 us (4%)
  local copies, waits for them, and re-layouts  18.8 us (3%)
  starting transfers between devices  17.7 us (3%)
  between operations  15.9 us (2%)
  matrix products  7.43 us (1%)
    psum x1, waiting for transfers between devices, shards(): lax.psum((grad_in, grad_out_t, grad_bin, grad_bout, level_part), ('lat',...  244 us
    unnamed x3, waiting for transfers between devices  242 us
    psum x1, blocking collectives, shards(): lax.psum((grad_in, grad_out_t, grad_bin, grad_bout, level_part), ('lat',...  75.9 us
    ppermute x4, starting transfers between devices, with_halo(): lax.ppermute(lax.slice_in_dim(block, 0, width, axis=dim), axis, backward)  15.7 us
  transfers between devices with their start and end apart: 10, of which 4 were waited for; matrix products, arithmetic and copies ran while one was open for 2% of the time, Pallas kernels for 0%

profile of v1, /device:TPU:2, one launch (start us, length us, event | category | flops | bytes accessed | tf_op | source)
XLA Modules:
  0.0 648.8 jit_solution(436478011480141905)
XLA Ops:
  7.2 0.7 convert_bitcast_fusion
  7.9 1.2 pad_maximum_fusion.23
  9.1 1.7 collective-permute-start
  10.8 4.1 collective-permute-start.1
  14.9 2.1 collective-permute-done
  16.9 1.2 pad_maximum_fusion
  18.1 1.2 fusion.831
  19.3 1.5 copy.1020
  20.9 0.4 copy.1021
  21.3 4.3 collective-permute-start.3
  25.6 0.8 collective-permute-done.2
  26.5 0.5 copy.1022
  26.9 0.5 copy.1023
  27.4 0.4 copy-done.2
  27.8 0.9 copy-done.3
  28.8 0.2 fusion.7
  29.2 0.2 copy-done.13
  29.4 2.3 fusion.735
  31.7 0.3 dynamic-update-slice
  32.0 0.6 copy-done.12
  32.7 0.2 all-reduce.12.cloned.1.call-start
  32.9 3.3 fusion.15
  36.3 0.8 copy.1030
  37.1 242.1 %all-reduce.10.cloned.1.call-done = f32[25600]{0:T(1024)} async-done(((f32[25600]{0:T(1024)}), f32[25600]{0:T(1024)}) %all-reduce.10.cloned.1.call-update) | async-done | bytes 102416
  279.2 1.1 reshape.55
  280.5 1.9 fusion.5
  282.4 0.6 compare_select_fusion
  283.1 0.3 add_add_fusion
  283.5 0.3 multiply_subtract_fusion.9
  283.9 0.5 fusion.146
  284.6 0.3 fusion.148
  284.9 0.3 fusion.49
  285.2 0.4 constant_dynamic-update-slice_fusion.199
  286.0 0.7 constant_dynamic-update-slice_fusion.162
  287.5 0.3 multiply_subtract_fusion.147
  287.9 0.5 bitcast_subtract_fusion.33
  288.6 0.3 fusion.411
  288.9 0.3 fusion.345
  289.2 0.4 constant_dynamic-update-slice_fusion.298
  290.0 0.7 constant_dynamic-update-slice_fusion.262
  291.5 0.2 subtract_multiply_fusion
  291.9 0.3 copy-done.4
  292.2 0.2 convert_reduce_fusion.1
  292.4 1.0 fusion.834
  293.4 1.1 convert_reduce_fusion
  294.5 1.0 copy-done.11
  295.5 1.0 fusion.543
  296.5 1.8 multiply_reduce_fusion
  298.3 3.5 collective-permute-start.4
  301.8 75.9 %all-reduce.5 = (f32[100]{0:T(128)S(1)}, f32[1,512]{1,0:T(1,128)S(1)}, f32[100]{0:T(128)S(1)}) all-reduce(f32[100]{0:T(128)S(1)} %get-tuple-element.826, f32[1,512]{1,0:T(1,128)S(1)} %bitcast.5569, f32[100]{0:T(128)S(1)} %get-tuple-element.15), channel_id=1, replica_groups=mesh['lat'=8,'lon'=32] {'lat','lon'}, use_global_device_ids=true, to_apply=%region_3.4 | all-reduce | flops 712 | bytes 5696 | tf_op jit(solution)/shard_map/psum | solution.py:140
  377.7 0.9 multiply_subtract_fusion
  378.6 0.6 broadcast_multiply_fusion.2
  379.4 1.4 fusion.832
  380.8 1.5 copy.1024
  382.3 1.5 copy.1026
  383.8 3.9 collective-permute-start.7
  387.7 0.5 broadcast_multiply_fusion.3
  388.2 1.9 copy.1033
  390.1 0.4 copy.1025
  390.5 1.3 copy.1027
  391.8 3.1 fusion.9
  394.9 243.8 %all-reduce.12.cloned.1.call-done = (f32[100,512]{1,0:T(8,128)}, f32[100,512]{1,0:T(8,128)}) async-done(((f32[100,512]{1,0:T(8,128)}, f32[100,512]{1,0:T(8,128)}), (f32[100,512]{1,0:T(8,128)}, f32[100,512]{1,0:T(8,128)})) %all-reduce.12.cloned.1.call-update) | async-done | bytes 409616 | tf_op jit(solution)/shard_map/psum | solution.py:140
  638.7 1.6 broadcast_multiply_fusion.1
  640.4 1.6 multiply_bitcast_fusion
  (258 shorter events, 2.6 us)
Async XLA Ops:
  7.2 273.3 %copy-start = (bf16[100,512]{1,0:T(8,128)(2,1)S(1)}, bf16[100,512]{1,0:T(8,128)(2,1)}, u32[]{:S(2)}) copy-start(bf16[100,512]{1,0:T(8,128)(2,1)} %param.14) | copy-start | bytes 307204
  7.2 272.1 %all-reduce.10.cloned.1.call-start = ((), (), s32[]{:S(2)}) async-start(), calls=%async_computation | async-start | bytes 204800
  9.1 7.8 %collective-permute-start = (f32[101,1,128]{2,1,0:T(1,128)S(1)}, f32[101,1,128]{2,1,0:T(1,128)S(1)}, u32[]{:S(2)}, u32[]{:S(2)}) collective-permute-start(f32[101,1,128]{2,1,0:T(1,128)S(1)} %get-tuple-element.624), channel_id=1, source_target_pairs={{0,32},{32,64},{64,96},{96,128},{128,160},{160,192},{192,224},{224... | collective-permute-start | bytes 155144 | tf_op jit(solution)/shard_map/ppermute | solution.py:17
  10.8 6.2 collective-permute-start.1
  19.3 9.4 %copy-start.1 = (f32[100,8,128]{2,1,0:T(8,128)S(1)}, f32[100,8,128]{2,1,0:T(8,128)}, u32[]{:S(2)}) copy-start(f32[100,8,128]{2,1,0:T(8,128)} %param.9) | copy-start | bytes 1228804
  20.9 5.6 collective-permute-start.2
  21.3 5.6 collective-permute-start.3
  26.9 0.9 copy-start.2
  27.8 0.9 copy-start.3
  28.7 0.7 copy-start.13
  32.0 0.6 copy-start.12
  32.7 606.0 %all-reduce.12.cloned.1.call-start = ((), (), s32[]{:S(2)}) async-start(), calls=%async_computation.1 | async-start | bytes 851968 | tf_op jit(solution)/shard_map/psum | solution.py:140
  32.9 3.3 copy-start.9
  32.9 4.2 copy-start.10
  36.2 244.2 %copy-start.15 = (f32[512]{0:T(512)S(1)}, f32[512]{0:T(512)}, u32[]{:S(2)}) copy-start(f32[512]{0:T(512)} %param.15) | copy-start | bytes 6148
  280.5 1.9 copy-start.14
  280.5 1.9 copy-start.16
  283.4 1.0 copy-start.7
  286.0 2.4 copy-start.8
  291.4 0.8 copy-start.4
  293.4 2.1 copy-start.6
  294.5 1.0 copy-start.11
  296.5 82.7 %copy-start.5 = (f32[100,8,128]{2,1,0:T(8,128)S(1)}, f32[100,8,128]{2,1,0:T(8,128)}, u32[]{:S(2)}) copy-start(f32[100,8,128]{2,1,0:T(8,128)} %copy-done.4) | copy-start | bytes 1228804
  298.3 80.8 %collective-permute-start.4 = (f32[100,1,128]{2,1,0:T(1,128)S(1)}, f32[100,1,128]{2,1,0:T(1,128)S(1)}, u32[]{:S(2)}, u32[]{:S(2)}) collective-permute-start(f32[100,1,128]{2,1,0:T(1,128)S(1)} %get-tuple-element.627), channel_id=1, source_target_pairs={{32,0},{64,32},{96,64},{128,96},{160,128},{192,160},{224,192},{0,2... | collective-permute-start | bytes 153608 | tf_op jit(solution)/shard_map/ppermute | solution.py:20
  301.8 77.4 %collective-permute-start.5 = (f32[100,1,128]{2,1,0:T(1,128)S(1)}, f32[100,1,128]{2,1,0:T(1,128)S(1)}, u32[]{:S(2)}, u32[]{:S(2)}) collective-permute-start(f32[100,1,128]{2,1,0:T(1,128)S(1)} %get-tuple-element.626), channel_id=1, source_target_pairs={{0,32},{32,64},{64,96},{96,128},{128,160},{160,192},{192,224},{224... | collective-permute-start | bytes 153608 | tf_op jit(solution)/shard_map/ppermute | solution.py:17
  382.2 7.8 %collective-permute-start.6 = (f32[100,10,1]{0,1,2:T(8,128)S(1)}, f32[100,10,1]{0,1,2:T(8,128)S(1)}, u32[]{:S(2)}, u32[]{:S(2)}) collective-permute-start(f32[100,10,1]{0,1,2:T(8,128)S(1)} %copy.1024), channel_id=1, source_target_pairs={{0,1},{1,2},{2,3},{3,4},{4,5},{5,6},{6,7},{7,8},{8,9},{9,10},{10,1... | collective-permute-start | bytes 12008 | tf_op jit(solution)/shard_map/ppermute | solution.py:17
  383.8 6.7 %collective-permute-start.7 = (f32[100,10,1]{0,1,2:T(8,128)S(1)}, f32[100,10,1]{0,1,2:T(8,128)S(1)}, u32[]{:S(2)}, u32[]{:S(2)}) collective-permute-start(f32[100,10,1]{0,1,2:T(8,128)S(1)} %copy.1026), channel_id=1, source_target_pairs={{1,0},{2,1},{3,2},{4,3},{5,4},{6,5},{7,6},{8,7},{9,8},{10,9},{11,1... | collective-permute-start | bytes 12008 | tf_op jit(solution)/shard_map/ppermute | solution.py:20
Sparse Core Ops, SparseCore 0:
  32.8 246.3 all-reduce.9
  390.2 248.4 all-reduce.11
